TPU v7x, 32 devices: a whole 2x2x4 slice. The times are simulated.
32 devices in a mesh: gx: 4 (over z), gy: 8 (over y, x, core).
Axes of the slice: x: 2, y: 2, z: 4, core: 2. Of those that a mesh axis runs over, the one named last changes fastest.
Arguments:
- sensitivity: float32 [3, 262144], P(None, ('gx', 'gy')), may hold values from -24 to 24
- node_weight: float32 [262144], P(('gx', 'gy')), may hold values from 0.05 to 0.5
- dest_device: int32 [262144, 1], P(('gx', 'gy')), may hold values from 0 to 31; in each aligned block of 8192 rows (0 to 8191, 8192 to 16383, ...) at most 512 rows name the same one
- dest_cell: int32 [262144], P(('gx', 'gy')), may hold values from 0 to 131071
- box_owner: int32 [262144, 1], P(('gx', 'gy')), may hold values from 0 to 31; in each aligned block of 8192 rows (0 to 8191, 8192 to 16383, ...) at most 512 rows name the same one
- box_slot: int32 [262144], P(('gx', 'gy')), may hold values from 0 to 63
- stiffness: float32 [64, 256, 256], P('gx', 'gy'), may hold values from 0.5 to 2
- anchor: float32 [3, 64, 256, 256], P(None, 'gx', 'gy'), may hold values from 3 to 6
- coupling: float32 [9, 64, 256, 256], P(None, 'gx', 'gy'), may hold values from -1 to 1
Outputs:
- adjoint: float32 [3, 64, 256, 256], P(None, 'gx', 'gy')
- box_gradient: float32 [3, 2048], P(None, ('gx', 'gy'))
Inputs may be any that keep to these rules, and one draw needn't show every extreme that they name: `dest_device`: among the rows of one device, no deformation device is named more than 512 times, and in some device's rows one is named exactly 512 times. `box_owner`: among the rows of one device, no owner is named more than 512 times, and in some device's rows one is named exactly 512 times.
All inputs are finite; a program needn't handle non-finite values.
Results may differ from a plain program's by a relative error of at most 0.0003.
Values sent between devices are 32-bit elements; how exact they have to be, the bound alone decides.
A program may use at most 192 MiB of HBM per device.

v0:
```python
import jax
import jax.numpy as jnp
from jax import lax
from jax.sharding import PartitionSpec as P

BOX_DEV = 64
SWEEPS = 4


def extended(cells, sides, width):
    for axis, dim in sides:
        count = lax.axis_size(axis)
        ends = count - 1
        head = lax.slice_in_dim(cells, 0, width, axis=dim)
        tail = lax.slice_in_dim(cells, cells.shape[dim] - width, cells.shape[dim], axis=dim)
        cells = jnp.concatenate(
            [
                lax.ppermute(tail, axis, [(i, (i + 1) % count) for i in range(ends)]),
                cells,
                lax.ppermute(head, axis, [((i + 1) % count, i) for i in range(ends)]),
            ],
            axis=dim,
        )
    return cells


def neighbour_sum(padded):
    z_padded = jnp.pad(padded, ((0, 0), (0, 0), (0, 0), (1, 1)))
    middle = z_padded[:, 1:-1, 1:-1, :]
    total = z_padded[:, 2:, 1:-1, 1:-1] + z_padded[:, :-2, 1:-1, 1:-1]
    total = total + z_padded[:, 1:-1, 2:, 1:-1] + z_padded[:, 1:-1, :-2, 1:-1]
    return total + middle[..., 2:] + middle[..., :-2]


def apply_transposed(field, weighted_pad, stiff, anchor, coupling):
    blocks = coupling.reshape((3, 3) + coupling.shape[1:])
    mixing = jnp.sum(blocks * field[:, None], axis=0)
    return 6.0 * stiff[None] * field - neighbour_sum(weighted_pad) + mixing + anchor * field


def slot_ranks(target, num_targets):
    row_count = target.shape[0]
    block = 128
    num_blocks = row_count // block
    one_hot = (target[:, None] == jnp.arange(num_targets, dtype=jnp.int32)[None, :]).astype(
        jnp.float32
    )
    one_hot = one_hot.reshape(num_blocks, block, num_targets)
    lower = (
        jnp.arange(block, dtype=jnp.int32)[:, None] > jnp.arange(block, dtype=jnp.int32)[None, :]
    ).astype(jnp.float32)
    within = jnp.einsum(
        "ij,bjt->bit",
        lower,
        one_hot,
        precision=lax.Precision.HIGHEST,
        preferred_element_type=jnp.float32,
    )
    totals = jnp.sum(one_hot, axis=1)
    before = jnp.cumsum(totals, axis=0) - totals
    ranks = jnp.sum((within + before[:, None, :]) * one_hot, axis=2)
    return ranks.reshape(row_count).astype(jnp.int32)


def pack_rows(payload, send_slot, total_slots):
    return jnp.zeros((payload.shape[0], total_slots), jnp.float32).at[:, send_slot].set(payload)


def solve_sweeps(load, stiffness, anchor, coupling):
    diagonal = 6.0 * stiffness[None] + anchor + jnp.stack([coupling[0], coupling[4], coupling[8]])
    stiff_pad = extended(stiffness, (("gx", 0), ("gy", 1)), 1)
    adjoint = load / diagonal
    for sweep_idx in range(1, SWEEPS):
        field_pad = extended(adjoint, (("gx", 1), ("gy", 2)), 1)
        weighted = stiff_pad[None] * field_pad
        applied = apply_transposed(adjoint, weighted, stiffness, anchor, coupling)
        adjoint = adjoint + (load - applied) / diagonal
    return adjoint


def body(
    sensitivity,
    node_weight,
    dest_device,
    dest_cell,
    box_owner,
    box_slot,
    stiffness,
    anchor,
    coupling,
):
    devices = lax.axis_size("gx") * lax.axis_size("gy")
    row_count = sensitivity.shape[1]
    capacity = 2 * row_count // devices
    total_slots = devices * capacity
    size_x, size_y, size_z = stiffness.shape
    cells = size_x * size_y * size_z
    target = dest_device[:, 0]
    send_slot = target * capacity + slot_ranks(target, devices)
    cell_float = dest_cell.astype(jnp.float32)
    payload = jnp.concatenate([sensitivity, node_weight[None], cell_float[None]], axis=0)
    arrived = lax.all_to_all(
        pack_rows(payload, send_slot, total_slots),
        ("gx", "gy"),
        split_axis=1,
        concat_axis=1,
        tiled=True,
    )
    cell_ids = arrived[4].astype(jnp.int32)
    load = jnp.zeros((3, cells), jnp.float32).at[:, cell_ids].add(arrived[0:3])
    load = load.reshape(3, size_x, size_y, size_z)
    adjoint = solve_sweeps(load, stiffness, anchor, coupling)
    flat_field = adjoint.reshape(3, cells)
    slot_gradient = arrived[3][None] * flat_field[:, cell_ids]
    returned = lax.all_to_all(slot_gradient, ("gx", "gy"), split_axis=1, concat_axis=1, tiled=True)
    row_gradient = returned[:, send_slot]
    owner_ids = box_owner[:, 0]
    owner_slot = owner_ids * capacity + slot_ranks(owner_ids, devices)
    owner_payload = jnp.concatenate([row_gradient, box_slot.astype(jnp.float32)[None]], axis=0)
    at_owner = lax.all_to_all(
        pack_rows(owner_payload, owner_slot, total_slots),
        ("gx", "gy"),
        split_axis=1,
        concat_axis=1,
        tiled=True,
    )
    box_match = (
        at_owner[3].astype(jnp.int32)[:, None] == jnp.arange(BOX_DEV, dtype=jnp.int32)[None, :]
    ).astype(jnp.float32)
    box_gradient = jnp.dot(
        at_owner[0:3],
        box_match,
        precision=lax.Precision.HIGHEST,
        preferred_element_type=jnp.float32,
    )
    return (adjoint, box_gradient)


def solution(mesh):
    placed = (
        P(None, ("gx", "gy")),
        P(("gx", "gy")),
        P(("gx", "gy"), None),
        P(("gx", "gy")),
        P(("gx", "gy"), None),
        P(("gx", "gy")),
        P("gx", "gy", None),
        P(None, "gx", "gy", None),
        P(None, "gx", "gy", None),
    )
    return jax.shard_map(
        body,
        mesh=mesh,
        in_specs=placed,
        out_specs=(P(None, "gx", "gy", None), P(None, ("gx", "gy"))),
        check_vma=False,
    )
```

profile of v0, /device:TPU:0, one launch (start us, length us, event | category | flops | bytes accessed | tf_op | source)
XLA Modules:
  0.0 1193.1 jit_solution(12968718230906046091)
XLA Ops:
  0.7 1.1 convert_reduce_fusion.1
  1.9 1.3 fusion.40
  3.4 2.7 copy.54
  6.1 24.5 %scatter_custom_fusion = f32[5,16384]{0,1:T(8,128)} fusion(s32[8192]{0:T(1024)S(1)} %bitcast.72, f32[8192,5]{1,0:T(8,128)} %copy.54, f32[]{:T(128)} %constant.6.clone.1), kind=kCustom, calls=%fused_computation.15 | custom fusion | bytes 328192 | tf_op jit(solution)/shard_map/scatter | solution.py:66
  30.6 6.0 copy.55
  36.7 7.3 all-to-all-start
  44.0 3.7 collective-permute-start
  47.7 1.3 collective-permute-start.1
  49.0 2.6 fusion.48
  52.1 1.8 collective-permute-done
  53.9 0.9 constant_dynamic-update-slice_fusion.1
  54.8 1.7 collective-permute-start.2
  56.5 1.3 collective-permute-start.3
  57.8 1.8 all-to-all-done
  59.8 7.1 sort
  67.1 5.4 copy.56
  72.5 231.4 %scatter_custom_fusion.1 = f32[3,131072]{0,1:T(8,128)} fusion(s32[16384]{0:T(1024)S(1)} %get-tuple-element.2, f32[]{:T(128)} %constant.6.clone.1, f32[16384,3]{1,0:T(8,128)} %copy.56, s32[16384]{0:T(1024)S(1)} %broadcast_clamp_fusion.1), kind=kCustom, calls=%fused_computation.6 | custom fusion | flops 49152 | bytes 1573376 | tf_op jit(solution)/shard_map/scatter-add | solution.py:110
  304.0 38.4 %copy.57 = f32[3,16,32,256]{3,2,1,0:T(8,128)S(1)} copy(f32[3,16,32,256]{0,3,2,1:T(8,128)} %bitcast.13) | data formatting | bytes 3145728 | tf_op jit(solution)/shard_map/reshape | solution.py:111
  342.4 2.2 fusion.47
  344.7 1.3 collective-permute-start.4
  346.0 1.3 collective-permute-start.5
  347.4 0.8 collective-permute-done.4
  348.2 6.9 collective-permute-done.5
  355.2 2.6 collective-permute-start.6
  357.8 1.3 collective-permute-start.7
  359.1 0.9 multiply_reduce_fusion.2
  360.0 6.1 collective-permute-done.7
  366.1 0.4 maximum_multiply_fusion
  366.6 2.4 fusion.19
  369.0 2.7 collective-permute-start.8
  371.7 1.3 collective-permute-start.9
  373.0 0.4 fusion.41
  373.4 0.5 collective-permute-done.8
  373.9 4.3 collective-permute-done.9
  378.3 3.3 collective-permute-start.10
  381.6 1.3 collective-permute-start.11
  382.9 0.9 multiply_reduce_fusion.1
  383.9 2.0 collective-permute-done.11
  385.9 0.4 maximum_multiply_fusion.1
  386.3 2.6 fusion.27
  388.9 1.9 collective-permute-start.12
  390.8 1.3 collective-permute-start.13
  392.1 0.9 collective-permute-done.12
  393.0 4.3 collective-permute-done.13
  397.4 3.3 collective-permute-start.14
  400.7 1.3 collective-permute-start.15
  402.0 0.9 multiply_reduce_fusion
  403.0 1.8 collective-permute-done.15
  404.8 0.4 maximum_multiply_fusion.2
  405.2 3.5 fusion.35
  408.7 33.2 %copy.62 = f32[3,16,32,256]{0,3,2,1:T(8,128)} copy(f32[3,16,32,256]{3,2,1,0:T(8,128)} %fusion.35) | data formatting | bytes 3145728 | tf_op jit(solution)/shard_map/add | solution.py:77
  441.9 635.2 %gather_fusion = f32[16384,3]{1,0:T(8,128)} fusion(f32[3,131072]{0,1:T(8,128)} %bitcast.20, s32[16384]{0:T(1024)S(1)} %broadcast_clamp_fusion), kind=kCustom, calls=%fused_computation | custom fusion | bytes 458752 | tf_op jit(solution)/shard_map/gather | solution.py:114
  1077.1 5.3 copy.63
  1082.4 0.8 broadcast_multiply_fusion.1
  1083.2 12.1 %all-to-all-start.1 = ((f32[3,32,512]{2,0,1:T(4,128)}), f32[3,32,512]{2,0,1:T(4,128)S(1)}, u32[]{:S(2)}, u32[]{:S(2)}) async-start(f32[3,32,512]{2,0,1:T(4,128)} %broadcast_multiply_fusion.1), calls=%async_computation.1 | async-start | bytes 524288 | tf_op jit(solution)/shard_map/all_to_all | solution.py:115
  1095.4 10.5 all-to-all-done.1
  1105.9 4.8 copy.64
  1110.7 31.3 %gather_fusion.1 = f32[8192,3]{1,0:T(8,128)} fusion(f32[3,16384]{0,1:T(8,128)} %bitcast.58, s32[8192]{0:T(1024)S(1)} %broadcast_clamp_fusion.2), kind=kCustom, calls=%fused_computation.1 | custom fusion | bytes 229376 | tf_op jit(solution)/shard_map/gather | solution.py:116
  1142.0 2.8 copy.65
  1144.9 2.7 copy.66
  1147.6 24.5 %scatter_custom_fusion.2 = f32[4,16384]{0,1:T(8,128)} fusion(s32[8192]{0:T(1024)S(1)} %bitcast.79, f32[8192,4]{1,0:T(8,128)} %copy.66, f32[]{:T(128)} %constant.6.clone.1), kind=kCustom, calls=%fused_computation.13 | custom fusion | bytes 262656 | tf_op jit(solution)/shard_map/scatter | solution.py:66
  1172.1 5.3 copy.67
  1177.4 12.8 %all_to_all.27 = f32[4,32,512]{2,0,1:T(4,128)S(1)} all-to-all(f32[4,32,512]{2,0,1:T(4,128)S(1)} %copy.67), channel_id=1, replica_groups=mesh['gx'=4,'gy'=8] {'gx','gy'}, dimensions={1} | all-to-all | bytes 524288 | tf_op jit(solution)/shard_map/all_to_all | solution.py:120
  1190.3 2.6 fusion.10
  (72 shorter events, 1.7 us)
Async XLA Ops:
  0.6 2.6 copy-start.9
  0.6 2.6 copy-start.12
  0.7 2.7 copy-start.11
  0.7 2.7 copy-start.8
  30.6 13.4 %copy-start.7 = (f32[16,32,256]{2,1,0:T(8,128)S(1)}, f32[16,32,256]{2,1,0:T(8,128)}, u32[]{:S(2)}) copy-start(f32[16,32,256]{2,1,0:T(8,128)} %param.15) | copy-start | bytes 1572868
  36.7 22.9 %all-to-all-start = ((f32[5,32,512]{2,0,1:T(8,128)}), f32[5,32,512]{2,0,1:T(8,128)S(1)}, u32[]{:S(2)}, u32[]{:S(2)}) async-start(f32[5,32,512]{2,0,1:T(8,128)} %copy.55), calls=%async_computation | async-start | bytes 1048576 | tf_op jit(solution)/shard_map/all_to_all | solution.py:102
  44.0 9.8 collective-permute-start
  47.7 3.9 copy-start.10
  47.7 7.0 collective-permute-start.1
  54.7 1.8 copy-start.5
  54.8 292.5 %collective-permute-start.2 = (f32[18,1,256]{2,1,0:T(1,128)S(1)}, f32[18,1,256]{2,1,0:T(1,128)S(1)}, u32[]{:S(2)}, u32[]{:S(2)}) collective-permute-start(f32[18,1,256]{2,1,0:T(1,128)S(1)} %get-tuple-element.19), channel_id=1, source_target_pairs={{0,1},{1,2},{2,3},{3,4},{4,5},{5,6},{6,7},{8,9},{9,10},{10,11},{11... | collective-permute-start | bytes 55304 | tf_op jit(solution)/shard_map/ppermute | solution.py:18
  56.5 290.8 %collective-permute-start.3 = (f32[18,1,256]{2,1,0:T(1,128)S(1)}, f32[18,1,256]{2,1,0:T(1,128)S(1)}, u32[]{:S(2)}, u32[]{:S(2)}) collective-permute-start(f32[18,1,256]{2,1,0:T(1,128)S(1)} %get-tuple-element.20), channel_id=1, source_target_pairs={{1,0},{2,1},{3,2},{4,3},{5,4},{6,5},{7,6},{9,8},{10,9},{11,10},{12... | collective-permute-start | bytes 55304 | tf_op jit(solution)/shard_map/ppermute | solution.py:20
  303.9 38.5 %copy-start = (f32[3,16,32,256]{3,2,1,0:T(8,128)S(1)}, f32[3,16,32,256]{3,2,1,0:T(8,128)}, u32[]{:S(2)}) copy-start(f32[3,16,32,256]{3,2,1,0:T(8,128)} %param.16) | copy-start | bytes 4718596
  342.4 16.7 %slice-start = ((s8[4718592]{0:T(1024)(128)(4,1)}), s8[4194304]{0:T(1024)(128)(4,1)S(1)}, s32[]{:S(2)}) async-start(s8[4718592]{0:T(1024)(128)(4,1)} %bitcast.51), calls=%async_computation.3 | async-start | bytes 8388608
  342.4 4.9 copy-start.6
  342.4 16.6 %slice-start.1 = ((s8[4718592]{0:T(1024)(128)(4,1)}), s8[524288]{0:T(1024)(128)(4,1)S(1)}, s32[]{:S(2)}) async-start(s8[4718592]{0:T(1024)(128)(4,1)} %bitcast.51), calls=%async_computation.4 | async-start | bytes 1048576
  344.7 3.5 collective-permute-start.4
  346.0 9.1 collective-permute-start.5
  355.2 4.9 collective-permute-start.6
  357.8 8.4 collective-permute-start.7
  360.0 6.5 copy-start.1
  360.0 6.5 copy-start.2
  360.0 6.5 copy-start.3
  360.0 6.5 copy-start.4
  369.0 4.9 collective-permute-start.8
  371.7 6.5 collective-permute-start.9
  378.3 5.5 collective-permute-start.10
  381.6 4.2 collective-permute-start.11
  388.9 4.1 collective-permute-start.12
  390.8 6.5 collective-permute-start.13
  397.4 5.5 collective-permute-start.14
  400.7 4.0 collective-permute-start.15
  1077.1 18.2 %copy-start.13 = (s32[8192]{0:T(1024)S(1)}, s32[8192]{0:T(1024)}, u32[]{:S(2)}) copy-start(s32[8192]{0:T(1024)} %param.14) | copy-start | bytes 98308
  1083.2 22.7 %all-to-all-start.1 = ((f32[3,32,512]{2,0,1:T(4,128)}), f32[3,32,512]{2,0,1:T(4,128)S(1)}, u32[]{:S(2)}, u32[]{:S(2)}) async-start(f32[3,32,512]{2,0,1:T(4,128)} %broadcast_multiply_fusion.1), calls=%async_computation.1 | async-start | bytes 524288 | tf_op jit(solution)/shard_map/all_to_all | solution.py:115
where the time goes:
time: 1200 us; the launch traced here: 1190 us
  local copies, waits for them, and re-layouts  825 us (69%)
  other arithmetic  257 us (21%)
  starting transfers between devices  50.2 us (4%)
  waiting for transfers between devices  41.6 us (3%)
  blocking collectives  12.8 us (1%)
    gather x2, local copies, waits for them, and re-layouts, body(): slot_gradient = arrived[3][None] * flat_field[:, cell_ids]  641 us
    scatter-add x3, other arithmetic, body(): load = jnp.zeros((3, cells), jnp.float32).at[:, cell_ids].add(arrived[0:3])  239 us
    scatter x2, local copies, waits for them, and re-layouts, pack_rows(): jnp.zeros((payload.shape[0], total_slots), jnp.float32).at[:, send_slot]  49.1 us
    reshape x1, local copies, waits for them, and re-layouts, body(): load = load.reshape(3, size_x, size_y, size_z)  38.4 us
    gather x2, local copies, waits for them, and re-layouts, body(): row_gradient = returned[:, send_slot]  34.1 us
    add x1, local copies, waits for them, and re-layouts, solve_sweeps(): adjoint = adjoint + (load - applied) / diagonal  33.2 us
    ppermute x8, waiting for transfers between devices, extended(): lax.ppermute(head, axis, [((i + 1) % count, i) for i in range(ends)])  25.4 us
  transfers between devices with their start and end apart: 18, of which 12 were waited for; matrix products, arithmetic and copies ran while one was open for 24% of the time, Pallas kernels for 0%

commit v1 on v0

v1 whole, which is shorter than its diff:
```python
import functools

import jax
import jax.numpy as jnp
from jax import lax
from jax.experimental import pallas as pl
from jax.experimental.pallas import tpu as pltpu
from jax.sharding import PartitionSpec as P

BOX_DEV = 64
SWEEPS = 4
NT = (((1,), (1,)), ((), ()))
F32 = jnp.float32
BF16 = jnp.bfloat16
MESH = pl.DeviceIdType.MESH


def two_terms(x):
    hi = x.astype(BF16).astype(F32)
    return hi, x - hi


def matches(count, row):
    return lax.broadcasted_iota(jnp.int32, (count, row.shape[1]), 0) == row


def one_hot(mask):
    return jnp.where(mask, 1.0, 0.0).astype(BF16)


def scaled(mask, row):
    return jnp.where(mask, row, 0.0).astype(BF16)


def dot_nt(a, b):
    return lax.dot_general(a, b, NT, preferred_element_type=F32)


def pack_kernel(size_z, step, sens, weight, device, cell, owner, slot, out, tri, seen):
    targets, fields, capacity = out.shape
    rows = sens.shape[1]
    out[...] = jnp.zeros_like(out)
    seen[...] = jnp.zeros_like(seen)
    tri[...] = one_hot(
        lax.broadcasted_iota(jnp.int32, (step, step), 0)
        < lax.broadcasted_iota(jnp.int32, (step, step), 1)
    )

    def block(index, carry):
        span = pl.ds(pl.multiple_of(index * step, step), step)
        target = device[:, span]
        chosen = matches(targets, target)
        before = jnp.dot(one_hot(chosen), tri[...], preferred_element_type=F32) + seen[:, :1]
        rank = jnp.sum(jnp.where(chosen, before, 0.0), axis=0, keepdims=True).astype(jnp.int32)
        seen[...] = seen[...] + jnp.sum(jnp.where(chosen, 1.0, 0.0), axis=1, keepdims=True)
        place = one_hot(matches(capacity, rank))
        cells = cell[:, span]
        payload = jnp.concatenate(
            [
                sens[:, span],
                weight[:, span],
                (cells % size_z).astype(F32),
                (cells // size_z).astype(F32),
                owner[:, span].astype(F32),
                slot[:, span].astype(F32),
            ],
            axis=0,
        )
        wide = (targets, fields, step)
        to = lax.broadcasted_iota(jnp.int32, wide, 0) == target[None]
        total = jnp.zeros((targets * fields, capacity), F32)
        for term in two_terms(payload):
            lhs = jnp.where(to, term[None], 0.0).reshape(targets * fields, step).astype(BF16)
            total = total + dot_nt(lhs, place)
        out[...] = out[...] + total.reshape(targets, fields, capacity)
        return carry

    lax.fori_loop(0, rows // step, block, 0)


def pack_rows(size_z, devices, capacity, sens, weight, device, cell, owner, slot):
    step = min(512, sens.shape[1])
    return pl.pallas_call(
        functools.partial(pack_kernel, size_z, step),
        out_shape=jax.ShapeDtypeStruct((devices, 8, capacity), F32),
        in_specs=[pl.BlockSpec(memory_space=pltpu.VMEM)] * 6,
        out_specs=pl.BlockSpec(memory_space=pltpu.VMEM),
        scratch_shapes=[pltpu.VMEM((step, step), BF16), pltpu.VMEM((devices, 128), F32)],
        name="pack_rows",
    )(sens, weight, device, cell, owner, slot)


def joined(ref):
    return jnp.concatenate([ref[i] for i in range(ref.shape[0])], axis=1)


def scatter_kernel(arrived, load):
    parts, size_xy, size_z = load.shape

    @pl.when(pl.program_id(0) == 0)
    def _():
        load[...] = jnp.zeros_like(load)

    block = joined(arrived)
    at_z = matches(size_z, block[4:5].astype(jnp.int32))
    at_xy = one_hot(matches(size_xy, block[5:6].astype(jnp.int32)))
    for k in range(parts):
        hi, lo = two_terms(block[k : k + 1])
        load[k] = load[k] + dot_nt(at_xy, scaled(at_z, hi)) + dot_nt(at_xy, scaled(at_z, lo))


def scatter_rows(arrived, group, size_xy, size_z):
    devices, fields, capacity = arrived.shape
    return pl.pallas_call(
        scatter_kernel,
        grid=(devices // group,),
        out_shape=jax.ShapeDtypeStruct((3, size_xy, size_z), F32),
        in_specs=[pl.BlockSpec((group, fields, capacity), lambda i: (i, 0, 0))],
        out_specs=pl.BlockSpec((3, size_xy, size_z), lambda i: (0, 0, 0)),
        name="scatter_rows",
    )(arrived)


def gather_kernel(arrived, field, boxes, terms):
    parts, size_xy, size_z = field.shape
    devices = boxes.shape[0]

    @pl.when(pl.program_id(0) == 0)
    def _():
        boxes[...] = jnp.zeros_like(boxes)
        for k in range(parts):
            hi, lo = two_terms(field[k].T)
            terms[k, :, :size_xy] = hi.astype(BF16)
            terms[k, :, size_xy:] = lo.astype(BF16)

    block = joined(arrived)
    at_z = matches(size_z, block[4:5].astype(jnp.int32))
    at_xy = one_hot(matches(size_xy, block[5:6].astype(jnp.int32)))
    twice = jnp.concatenate([at_xy, at_xy], axis=0)
    at_owner = one_hot(matches(devices, block[6:7].astype(jnp.int32)))
    at_slot = matches(BOX_DEV, block[7:8].astype(jnp.int32))
    for k in range(parts):
        column = jnp.dot(terms[k], twice, preferred_element_type=F32)
        value = jnp.sum(jnp.where(at_z, column, 0.0), axis=0, keepdims=True) * block[3:4]
        hi, lo = two_terms(value)
        part = dot_nt(at_owner, scaled(at_slot, hi)) + dot_nt(at_owner, scaled(at_slot, lo))
        boxes[:, k * BOX_DEV : (k + 1) * BOX_DEV] += part


def gather_rows(arrived, group, field):
    devices, fields, capacity = arrived.shape
    parts, size_xy, size_z = field.shape
    return pl.pallas_call(
        gather_kernel,
        grid=(devices // group,),
        out_shape=jax.ShapeDtypeStruct((devices, 3 * BOX_DEV), F32),
        in_specs=[
            pl.BlockSpec((group, fields, capacity), lambda i: (i, 0, 0)),
            pl.BlockSpec(memory_space=pltpu.VMEM),
        ],
        out_specs=pl.BlockSpec((devices, 3 * BOX_DEV), lambda i: (0, 0)),
        scratch_shapes=[pltpu.VMEM((parts, size_z, 2 * size_xy), BF16)],
        name="gather_rows",
    )(arrived, field)


def sweep_kernel(load, stiff, anchor, coupling, adjoint, weighted, rest, inverse, edge, halo, x_send, x_recv, y_send, y_recv):
    parts, size_x, size_y, size_z = load.shape
    exchanges = weighted.shape[0]
    gx, gy = lax.axis_index("gx"), lax.axis_index("gy")
    last_x, last_y = lax.axis_size("gx") - 1, lax.axis_size("gy") - 1
    sides = (("gx", gx, -1, gx > 0), ("gx", gx, 1, gx < last_x), ("gy", gy, -1, gy > 0), ("gy", gy, 1, gy < last_y))
    y_at = lax.broadcasted_iota(jnp.int32, (size_y, size_z), 0)
    z_at = lax.broadcasted_iota(jnp.int32, (size_y, size_z), 1)

    for index in range(exchanges):
        for k in range(parts):
            weighted[index, k, 0] = jnp.zeros((size_y, size_z), F32)
            weighted[index, k, size_x + 1] = jnp.zeros((size_y, size_z), F32)
    halo[...] = jnp.zeros_like(halo)

    barrier = pltpu.get_barrier_semaphore()
    known = 0
    for axis, place, move, present in sides:
        known = known + present.astype(jnp.int32)

        @pl.when(present)
        def _():
            pl.semaphore_signal(barrier, inc=1, device_id={axis: place + move}, device_id_type=MESH)

    pl.semaphore_wait(barrier, known)

    def copies(index):
        made = []
        for side, (axis, place, move, present) in enumerate(sides):
            there = 1 - side % 2
            if axis == "gx":
                pair = (weighted.at[index, :, 1 if move < 0 else size_x], weighted.at[index, :, size_x + 1 if move < 0 else 0])
                sems = (x_send, x_recv)
            else:
                pair = (edge.at[index, side % 2], halo.at[index, there])
                sems = (y_send, y_recv)
            made.append((present, pltpu.make_async_remote_copy(
                src_ref=pair[0],
                dst_ref=pair[1],
                send_sem=sems[0].at[index, side % 2],
                recv_sem=sems[1].at[index, there],
                device_id={axis: place + move},
                device_id_type=MESH,
            )))
        return made

    def arrivals(index):
        made = []
        for side, (axis, place, move, present) in enumerate(sides):
            if axis == "gx":
                pair = (weighted.at[index, :, 1 if move < 0 else size_x], weighted.at[index, :, 0 if move < 0 else size_x + 1])
                sems = (x_send, x_recv)
            else:
                pair = (edge.at[index, side % 2], halo.at[index, side % 2])
                sems = (y_send, y_recv)
            made.append((present, pltpu.make_async_remote_copy(
                src_ref=pair[0],
                dst_ref=pair[1],
                send_sem=sems[0].at[index, side % 2],
                recv_sem=sems[1].at[index, side % 2],
                device_id={axis: place + move},
                device_id_type=MESH,
            )))
        return made

    def publish(index, x, k, value):
        adjoint[k, x] = value
        if index < exchanges:
            product = stiff[x] * value
            weighted[index, k, x + 1] = product
            edge[index, 0, k, pl.ds(x, 1), :] = product[0:1]
            edge[index, 1, k, pl.ds(x, 1), :] = product[size_y - 1 : size_y]

    def first(x, carry):
        for k in range(parts):
            inverse[k, x] = 1.0 / (6.0 * stiff[x] + anchor[k, x] + coupling[4 * k, x])
            publish(0, x, k, load[k, x] * inverse[k, x])
        return carry

    lax.fori_loop(0, size_x, first, 0)
    for index in range(exchanges):
        for present, copy in copies(index):

            @pl.when(present)
            def _():
                copy.start()

        def near(x, carry):
            fields = [adjoint[k, x] for k in range(parts)]
            for k in range(parts):
                product = weighted[index, k, x + 1]
                value = load[k, x] - 6.0 * product - anchor[k, x] * fields[k]
                for j in range(parts):
                    value = value - coupling[3 * j + k, x] * fields[j]
                value = value + jnp.where(z_at == 0, 0.0, pltpu.roll(product, 1, 1))
                value = value + jnp.where(z_at == size_z - 1, 0.0, pltpu.roll(product, size_z - 1, 1))
                value = value + jnp.where(y_at == 0, 0.0, pltpu.roll(product, 1, 0))
                value = value + jnp.where(y_at == size_y - 1, 0.0, pltpu.roll(product, size_y - 1, 0))
                rest[k, x] = value
            return carry

        lax.fori_loop(0, size_x, near, 0)
        for present, copy in arrivals(index):

            @pl.when(present)
            def _():
                copy.wait_recv()

        def far(x, carry):
            for k in range(parts):
                value = rest[k, x] + weighted[index, k, x] + weighted[index, k, x + 2]
                value = value + jnp.where(y_at == 0, halo[index, 0, k, pl.ds(x, 1), :], 0.0)
                value = value + jnp.where(y_at == size_y - 1, halo[index, 1, k, pl.ds(x, 1), :], 0.0)
                publish(index + 1, x, k, adjoint[k, x] + value * inverse[k, x])
            return carry

        lax.fori_loop(0, size_x, far, 0)
    for index in range(exchanges):
        for present, copy in copies(index):

            @pl.when(present)
            def _():
                copy.wait_send()


def solve_sweeps(load, stiffness, anchor, coupling):
    parts, size_x, size_y, size_z = load.shape
    exchanges = SWEEPS - 1
    return pl.pallas_call(
        sweep_kernel,
        out_shape=jax.ShapeDtypeStruct(load.shape, F32),
        in_specs=[pl.BlockSpec(memory_space=pltpu.VMEM)] * 4,
        out_specs=pl.BlockSpec(memory_space=pltpu.VMEM),
        scratch_shapes=[
            pltpu.VMEM((exchanges, parts, size_x + 2, size_y, size_z), F32),
            pltpu.VMEM(load.shape, F32),
            pltpu.VMEM(load.shape, F32),
            pltpu.VMEM((exchanges, 2, parts, size_x, size_z), F32),
            pltpu.VMEM((exchanges, 2, parts, size_x, size_z), F32),
        ]
        + [pltpu.SemaphoreType.DMA((exchanges, 2))] * 4,
        compiler_params=pltpu.CompilerParams(collective_id=0, has_side_effects=True),
        name="sweeps",
    )(load, stiffness, anchor, coupling)


def body(
    sensitivity,
    node_weight,
    dest_device,
    dest_cell,
    box_owner,
    box_slot,
    stiffness,
    anchor,
    coupling,
):
    devices = lax.axis_size("gx") * lax.axis_size("gy")
    row_count = sensitivity.shape[1]
    capacity = 2 * row_count // devices
    size_x, size_y, size_z = stiffness.shape
    size_xy = size_x * size_y
    group = max(1, min(devices, 512 // capacity))

    def row(values):
        return values.reshape(1, row_count)

    packed = pack_rows(
        size_z,
        devices,
        capacity,
        sensitivity,
        row(node_weight),
        row(dest_device),
        row(dest_cell),
        row(box_owner),
        row(box_slot),
    )
    arrived = lax.all_to_all(packed, ("gx", "gy"), split_axis=0, concat_axis=0, tiled=True)
    load = scatter_rows(arrived, group, size_xy, size_z)
    load = load.reshape(3, size_x, size_y, size_z)
    adjoint = solve_sweeps(load, stiffness, anchor, coupling)
    partial = gather_rows(arrived, group, adjoint.reshape(3, size_xy, size_z))
    partial = lax.all_to_all(partial, ("gx", "gy"), split_axis=0, concat_axis=0, tiled=True)
    box_gradient = jnp.sum(partial, axis=0).reshape(3, BOX_DEV)
    return (adjoint, box_gradient)


def solution(mesh):
    placed = (
        P(None, ("gx", "gy")),
        P(("gx", "gy")),
        P(("gx", "gy"), None),
        P(("gx", "gy")),
        P(("gx", "gy"), None),
        P(("gx", "gy")),
        P("gx", "gy", None),
        P(None, "gx", "gy", None),
        P(None, "gx", "gy", None),
    )
    return jax.shard_map(
        body,
        mesh=mesh,
        in_specs=placed,
        out_specs=(P(None, "gx", "gy", None), P(None, ("gx", "gy"))),
        check_vma=False,
    )
```

time: 1200 us -> 161 us (0.13)
  local copies, waits for them, and re-layouts: 825 us -> 2.6 us
  other arithmetic: 257 us -> 0.06 us
  Pallas kernels: 0 us -> 124 us
  starting transfers between devices: 50.2 us -> 0 us
  waiting for transfers between devices: 41.6 us -> 0 us
  blocking collectives: 12.8 us -> 33.4 us
    gather x4 -> x0, local copies, waits for them, and re-layouts: 675 us -> none  [the longest x2 641 us: body(): slot_gradient = arrived[3][None] * flat_field[:, cell_ids]]
    scatter-add x3 -> x0, other arithmetic: 239 us -> none  [body(): load = jnp.zeros((3, cells), jnp.float32).at[:, cell_ids].add(arrived[0:3])]
    pallas_call x0 -> x4, Pallas kernels: none -> 124 us  [the longest x1 55.6 us: gather_rows(): pl.pallas_call(gather_kernel, grid=(devices // group,), out_shape=jax.Sha...]
    scatter x2 -> x0, local copies, waits for them, and re-layouts: 49.1 us -> none  [pack_rows(): jnp.zeros((payload.shape[0], total_slots), jnp.float32).at[:, send_slot]]
    reshape x1, local copies, waits for them, and re-layouts: 38.4 us -> 0.66 us  [body(): box_gradient = jnp.sum(partial, axis=0).reshape(3, BOX_DEV)]
    add x1 -> x0, local copies, waits for them, and re-layouts: 33.2 us -> none  [solve_sweeps(): adjoint = adjoint + (load - applied) / diagonal]
    ppermute x16 -> x0, starting transfers between devices: 30.8 us -> none  [the longest x8 20.5 us: extended(): lax.ppermute(tail, axis, [(i, (i + 1) % count) for i in range(ends)])]
    ppermute x16 -> x0, waiting for transfers between devices: 29.3 us -> none  [the longest x8 25.4 us: extended(): lax.ppermute(head, axis, [((i + 1) % count, i) for i in range(ends)])]
  transfers between devices with their start and end apart: 18 -> 0, of which waited for: 12 -> 0; matrix products, arithmetic and copies ran while one was open for 24% -> 0% of each run, Pallas kernels for 0% -> 0%
where the time goes in v1:
time: 161 us; the launch traced here: 160 us
  Pallas kernels  124 us (77%)
  blocking collectives  33.4 us (21%)
  local copies, waits for them, and re-layouts  2.6 us (2%)
    pallas_call x1, Pallas kernels, gather_rows(): pl.pallas_call(gather_kernel, grid=(devices // group,), out_shape=jax.Sha...  55.6 us
    pallas_call x1, Pallas kernels, scatter_rows(): pl.pallas_call(scatter_kernel, grid=(devices // group,), out_shape=jax.Sh...  35.4 us
    all_to_all x1, blocking collectives, body(): lax.all_to_all(packed, ('gx', 'gy'), split_axis=0, concat_axis=0, tiled=T...  23.1 us
    pallas_call x1, Pallas kernels, solve_sweeps(): pl.pallas_call(sweep_kernel, out_shape=jax.ShapeDtypeStruct(load.shape, F...  19.4 us
    pallas_call x1, Pallas kernels, pack_rows(): pl.pallas_call(functools.partial(pack_kernel, size_z, step), out_shape=ja...  13.2 us
    all_to_all x1, blocking collectives, body(): lax.all_to_all(partial, ('gx', 'gy'), split_axis=0, concat_axis=0, tiled=...  10.3 us

profile of v1, /device:TPU:0, one launch (start us, length us, event | category | flops | bytes accessed | tf_op | source)
XLA Modules:
  0.0 160.3 jit_solution(13378391799777527236)
XLA Ops:
  0.6 13.2 %pack_rows.1 = f32[32,8,512]{2,1,0:T(8,128)} custom-call(f32[3,8192]{1,0:T(4,128)} %sens.1, f32[1,8192]{1,0:T(1,128)} %bitcast.11, s32[1,8192]{1,0:T(1,128)} %bitcast.12, s32[1,8192]{1,0:T(1,128)} %bitcast.13, s32[1,8192]{1,0:T(1,128)} %bitcast.14, s32[1,8192]{1,0:T(1,128)} %bitcast.15), custom_call_target="tpu_custom_call" | custom-call | tf_op jit(solution)/shard_map/pack_rows/pallas_call | solution.py:83
  13.8 23.1 %all_to_all.14.arrived = f32[32,8,512]{2,1,0:T(8,128)} all-to-all(f32[32,8,512]{2,1,0:T(8,128)} %pack_rows.1), channel_id=1, replica_groups=mesh['gx'=4,'gy'=8] {'gx','gy'}, dimensions={0} | all-to-all | bytes 1048576 | tf_op jit(solution)/shard_map/all_to_all | solution.py:345
  36.9 35.4 %scatter_rows.1 = f32[3,512,256]{2,1,0:T(8,128)} custom-call(f32[32,8,512]{2,1,0:T(8,128)} %all_to_all.14.arrived), custom_call_target="tpu_custom_call" | custom-call | tf_op jit(solution)/shard_map/scatter_rows/pallas_call | solution.py:114
  72.2 19.4 %sweeps.1 = f32[3,16,32,256]{3,2,1,0:T(8,128)} custom-call(f32[3,16,32,256]{3,2,1,0:T(8,128)} %bitcast.9, f32[16,32,256]{2,1,0:T(8,128)} %stiff.1, f32[3,16,32,256]{3,2,1,0:T(8,128)} %anchor.1, f32[9,16,32,256]{3,2,1,0:T(8,128)} %coupling.1), custom_call_target="tpu_custom_call" | custom-call | tf_op jit(solution)/shard_map/sweeps/pallas_call | solution.py:295
  91.7 0.0 copy-start
  91.7 55.6 %gather_rows.1 = f32[32,192]{1,0:T(8,128)} custom-call(f32[32,8,512]{2,1,0:T(8,128)} %all_to_all.14.arrived, f32[3,512,256]{2,1,0:T(8,128)} %bitcast.8), custom_call_target="tpu_custom_call" | custom-call | tf_op jit(solution)/shard_map/gather_rows/pallas_call | solution.py:153
  147.3 0.8 copy.11
  148.1 10.3 %all_to_all.15 = f32[32,1,192]{2,1,0:T(1,128)S(1)} all-to-all(f32[32,1,192]{2,1,0:T(1,128)S(1)} %copy.11), channel_id=1, replica_groups=mesh['gx'=4,'gy'=8] {'gx','gy'}, dimensions={0} | all-to-all | bytes 49152 | tf_op jit(solution)/shard_map/all_to_all | solution.py:350
  158.4 0.1 reduce_sum.9
  158.5 0.7 reshape.37
  159.1 0.0 copy-done
  159.1 1.1 copy.13
Async XLA Ops:
  91.7 67.5 %copy-start = (f32[3,16,32,256]{3,2,1,0:T(8,128)S(1)}, f32[3,16,32,256]{3,2,1,0:T(8,128)}, u32[]{:S(2)}) copy-start(f32[3,16,32,256]{3,2,1,0:T(8,128)} %sweeps.1) | copy-start | bytes 4718596

commit v2 on v1

--- a/solution.py
+++ b/solution.py
@@ -68,11 +68,13 @@
         )
         wide = (targets, fields, step)
         to = lax.broadcasted_iota(jnp.int32, wide, 0) == target[None]
-        total = jnp.zeros((targets * fields, capacity), F32)
-        for term in two_terms(payload):
-            lhs = jnp.where(to, term[None], 0.0).reshape(targets * fields, step).astype(BF16)
-            total = total + dot_nt(lhs, place)
-        out[...] = out[...] + total.reshape(targets, fields, capacity)
+        terms = [
+            jnp.where(to, term[None], 0.0).reshape(targets * fields, step).astype(BF16)
+            for term in two_terms(payload)
+        ]
+        product = dot_nt(jnp.concatenate(terms, axis=0), place)
+        product = product[: targets * fields] + product[targets * fields :]
+        out[...] = out[...] + product.reshape(targets, fields, capacity)
         return carry
 
     lax.fori_loop(0, rows // step, block, 0)
@@ -94,19 +96,26 @@
     return jnp.concatenate([ref[i] for i in range(ref.shape[0])], axis=1)
 
 
-def scatter_kernel(arrived, load):
+def scatter_kernel(arrived, load, total):
     parts, size_xy, size_z = load.shape
 
     @pl.when(pl.program_id(0) == 0)
     def _():
-        load[...] = jnp.zeros_like(load)
+        total[...] = jnp.zeros_like(total)
 
     block = joined(arrived)
     at_z = matches(size_z, block[4:5].astype(jnp.int32))
     at_xy = one_hot(matches(size_xy, block[5:6].astype(jnp.int32)))
-    for k in range(parts):
-        hi, lo = two_terms(block[k : k + 1])
-        load[k] = load[k] + dot_nt(at_xy, scaled(at_z, hi)) + dot_nt(at_xy, scaled(at_z, lo))
+    pairs = [two_terms(block[k : k + 1]) for k in range(parts)]
+    terms = [scaled(at_z, hi) for hi, lo in pairs] + [scaled(at_z, lo) for hi, lo in pairs]
+    product = dot_nt(jnp.concatenate(terms, axis=0), at_xy)
+    half = parts * size_z
+    total[...] = total[...] + product[:half] + product[half:]
+
+    @pl.when(pl.program_id(0) == pl.num_programs(0) - 1)
+    def _():
+        for k in range(parts):
+            load[k] = total[k * size_z : (k + 1) * size_z].T
 
 
 def scatter_rows(arrived, group, size_xy, size_z):
@@ -117,6 +126,7 @@
         out_shape=jax.ShapeDtypeStruct((3, size_xy, size_z), F32),
         in_specs=[pl.BlockSpec((group, fields, capacity), lambda i: (i, 0, 0))],
         out_specs=pl.BlockSpec((3, size_xy, size_z), lambda i: (0, 0, 0)),
+        scratch_shapes=[pltpu.VMEM((3 * size_z, size_xy), F32)],
         name="scatter_rows",
     )(arrived)
 
@@ -130,17 +140,18 @@
         boxes[...] = jnp.zeros_like(boxes)
         for k in range(parts):
             hi, lo = two_terms(field[k].T)
-            terms[k, :, :size_xy] = hi.astype(BF16)
-            terms[k, :, size_xy:] = lo.astype(BF16)
+            terms[k * size_z : (k + 1) * size_z] = hi.astype(BF16)
+            terms[(parts + k) * size_z : (parts + k + 1) * size_z] = lo.astype(BF16)
 
     block = joined(arrived)
     at_z = matches(size_z, block[4:5].astype(jnp.int32))
     at_xy = one_hot(matches(size_xy, block[5:6].astype(jnp.int32)))
-    twice = jnp.concatenate([at_xy, at_xy], axis=0)
+    columns = jnp.dot(terms[...], at_xy, preferred_element_type=F32)
     at_owner = one_hot(matches(devices, block[6:7].astype(jnp.int32)))
     at_slot = matches(BOX_DEV, block[7:8].astype(jnp.int32))
     for k in range(parts):
-        column = jnp.dot(terms[k], twice, preferred_element_type=F32)
+        column = columns[k * size_z : (k + 1) * size_z]
+        column = column + columns[(parts + k) * size_z : (parts + k + 1) * size_z]
         value = jnp.sum(jnp.where(at_z, column, 0.0), axis=0, keepdims=True) * block[3:4]
         hi, lo = two_terms(value)
         part = dot_nt(at_owner, scaled(at_slot, hi)) + dot_nt(at_owner, scaled(at_slot, lo))
@@ -159,7 +170,7 @@
             pl.BlockSpec(memory_space=pltpu.VMEM),
         ],
         out_specs=pl.BlockSpec((devices, 3 * BOX_DEV), lambda i: (0, 0)),
-        scratch_shapes=[pltpu.VMEM((parts, size_z, 2 * size_xy), BF16)],
+        scratch_shapes=[pltpu.VMEM((2 * parts * size_z, size_xy), BF16)],
         name="gather_rows",
     )(arrived, field)
 
@@ -310,6 +321,63 @@
     )(load, stiffness, anchor, coupling)
 
 
+def exchange_kernel(send, recv, send_sem, recv_sem, own_sem):
+    count = send.shape[0]
+    width = lax.axis_size("gy")
+    me = lax.axis_index("gx") * width + lax.axis_index("gy")
+    barrier = pltpu.get_barrier_semaphore()
+
+    def device(index):
+        return (index // width, index % width)
+
+    def greet(step, carry):
+        pl.semaphore_signal(barrier, inc=1, device_id=device((me + step) % count), device_id_type=MESH)
+        return carry
+
+    lax.fori_loop(1, count, greet, 0)
+    pl.semaphore_wait(barrier, count - 1)
+
+    def copy(step, source, landing):
+        peer = (me + step) % count
+        return pltpu.make_async_remote_copy(
+            src_ref=send.at[source],
+            dst_ref=recv.at[landing],
+            send_sem=send_sem.at[step],
+            recv_sem=recv_sem.at[step],
+            device_id=device(peer),
+            device_id_type=MESH,
+        )
+
+    def start(step, carry):
+        copy(step, (me + step) % count, me).start()
+        return carry
+
+    lax.fori_loop(1, count, start, 0)
+    own = pltpu.make_async_copy(send.at[me], recv.at[me], own_sem)
+    own.start()
+
+    def finish(step, carry):
+        copy(step, (me + step) % count, (me + count - step) % count).wait_recv()
+        copy(step, (me + step) % count, me).wait_send()
+        return carry
+
+    lax.fori_loop(1, count, finish, 0)
+    own.wait()
+
+
+def exchange(blocks, number):
+    count = blocks.shape[0]
+    return pl.pallas_call(
+        exchange_kernel,
+        out_shape=jax.ShapeDtypeStruct(blocks.shape, F32),
+        in_specs=[pl.BlockSpec(memory_space=pltpu.VMEM)],
+        out_specs=pl.BlockSpec(memory_space=pltpu.VMEM),
+        scratch_shapes=[pltpu.SemaphoreType.DMA((count,))] * 2 + [pltpu.SemaphoreType.DMA],
+        compiler_params=pltpu.CompilerParams(collective_id=number, has_side_effects=True),
+        name="exchange_" + str(number),
+    )(blocks)
+
+
 def body(
     sensitivity,
     node_weight,
@@ -342,13 +410,13 @@
         row(box_owner),
         row(box_slot),
     )
-    arrived = lax.all_to_all(packed, ("gx", "gy"), split_axis=0, concat_axis=0, tiled=True)
+    arrived = exchange(packed, 1)
     load = scatter_rows(arrived, group, size_xy, size_z)
     load = load.reshape(3, size_x, size_y, size_z)
     adjoint = solve_sweeps(load, stiffness, anchor, coupling)
     partial = gather_rows(arrived, group, adjoint.reshape(3, size_xy, size_z))
-    partial = lax.all_to_all(partial, ("gx", "gy"), split_axis=0, concat_axis=0, tiled=True)
-    box_gradient = jnp.sum(partial, axis=0).reshape(3, BOX_DEV)
+    partial = exchange(partial.reshape(devices, 1, 3 * BOX_DEV), 2)
+    box_gradient = jnp.sum(partial, axis=(0, 1)).reshape(3, BOX_DEV)
     return (adjoint, box_gradient)
 
 

time: 161 us -> 148 us (0.919)
  blocking collectives: 33.4 us -> 0 us
  Pallas kernels: 124 us -> 142 us
    all_to_all x2 -> x0, blocking collectives: 33.4 us -> none  [the longest x1 23.1 us: body(): lax.all_to_all(packed, ('gx', 'gy'), split_axis=0, concat_axis=0, tiled=T...]
    pallas_call x0 -> x2, Pallas kernels: none -> 28.9 us  [exchange(): pl.pallas_call(exchange_kernel, out_shape=jax.ShapeDtypeStruct(blocks.sha...]
    pallas_call x1, Pallas kernels: 55.6 us -> 42.2 us  [gather_rows(): pl.pallas_call(gather_kernel, grid=(devices // group,), out_shape=jax.Sha...]
    pallas_call x1, Pallas kernels: 19.4 us -> 22.9 us  [solve_sweeps(): pl.pallas_call(sweep_kernel, out_shape=jax.ShapeDtypeStruct(load.shape, F...]
where the time goes in v2:
time: 148 us; the launch traced here: 147 us
  Pallas kernels  142 us (96%)
  local copies, waits for them, and re-layouts  3.19 us (2%)
    pallas_call x1, Pallas kernels, gather_rows(): pl.pallas_call(gather_kernel, grid=(devices // group,), out_shape=jax.Sha...  42.2 us
    pallas_call x1, Pallas kernels, scatter_rows(): pl.pallas_call(scatter_kernel, grid=(devices // group,), out_shape=jax.Sh...  35.6 us
    pallas_call x2, Pallas kernels, exchange(): pl.pallas_call(exchange_kernel, out_shape=jax.ShapeDtypeStruct(blocks.sha...  28.9 us
    pallas_call x1, Pallas kernels, solve_sweeps(): pl.pallas_call(sweep_kernel, out_shape=jax.ShapeDtypeStruct(load.shape, F...  22.9 us
    pallas_call x1, Pallas kernels, pack_rows(): pl.pallas_call(functools.partial(pack_kernel, size_z, step), out_shape=ja...  12.9 us

profile of v2, /device:TPU:0, one launch (start us, length us, event | category | flops | bytes accessed | tf_op | source)
XLA Modules:
  0.0 147.1 jit_solution(6790067677085472444)
XLA Ops:
  0.6 12.9 %pack_rows.1.send = f32[32,8,512]{2,1,0:T(8,128)} custom-call(f32[3,8192]{1,0:T(4,128)} %sens.1, f32[1,8192]{1,0:T(1,128)} %bitcast.9, s32[1,8192]{1,0:T(1,128)} %bitcast.10, s32[1,8192]{1,0:T(1,128)} %bitcast.11, s32[1,8192]{1,0:T(1,128)} %bitcast.12, s32[1,8192]{1,0:T(1,128)} %bitcast.13), custom_call_target="tpu_custom_call" | custom-call | tf_op jit(solution)/shard_map/pack_rows/pallas_call | solution.py:85
  13.5 18.4 %exchange_1.1.arrived = f32[32,8,512]{2,1,0:T(8,128)} custom-call(f32[32,8,512]{2,1,0:T(8,128)} %pack_rows.1.send), custom_call_target="tpu_custom_call" | custom-call | tf_op jit(solution)/shard_map/exchange_1/pallas_call | solution.py:370
  31.9 35.6 %scatter_rows.1 = f32[3,512,256]{2,1,0:T(8,128)} custom-call(f32[32,8,512]{2,1,0:T(8,128)} %exchange_1.1.arrived), custom_call_target="tpu_custom_call" | custom-call | tf_op jit(solution)/shard_map/scatter_rows/pallas_call | solution.py:123
  67.5 22.9 %sweeps.1 = f32[3,16,32,256]{3,2,1,0:T(8,128)} custom-call(f32[3,16,32,256]{3,2,1,0:T(8,128)} %bitcast.8, f32[16,32,256]{2,1,0:T(8,128)} %stiff.1, f32[3,16,32,256]{3,2,1,0:T(8,128)} %anchor.1, f32[9,16,32,256]{3,2,1,0:T(8,128)} %coupling.1), custom_call_target="tpu_custom_call" | custom-call | tf_op jit(solution)/shard_map/sweeps/pallas_call | solution.py:306
  90.3 0.0 copy-start
  90.3 42.2 %gather_rows.1 = f32[32,192]{1,0:T(8,128)} custom-call(f32[32,8,512]{2,1,0:T(8,128)} %exchange_1.1.arrived, f32[3,512,256]{2,1,0:T(8,128)} %bitcast.7), custom_call_target="tpu_custom_call" | custom-call | tf_op jit(solution)/shard_map/gather_rows/pallas_call | solution.py:164
  132.6 1.4 reshape.38.send
  133.9 10.5 %exchange_2.1 = f32[32,1,192]{2,1,0:T(1,128)} custom-call(f32[32,1,192]{2,1,0:T(1,128)} %reshape.38.send), custom_call_target="tpu_custom_call" | custom-call | tf_op jit(solution)/shard_map/exchange_2/pallas_call | solution.py:370
  144.5 0.8 reduce_sum.9
  145.3 0.7 reshape.39
  145.9 0.0 copy-done
  145.9 1.1 copy.12
Async XLA Ops:
  90.3 55.6 %copy-start = (f32[3,16,32,256]{3,2,1,0:T(8,128)S(1)}, f32[3,16,32,256]{3,2,1,0:T(8,128)}, u32[]{:S(2)}) copy-start(f32[3,16,32,256]{3,2,1,0:T(8,128)} %sweeps.1) | copy-start | bytes 4718596

commit v3 on v2

--- a/solution.py
+++ b/solution.py
@@ -9,6 +9,7 @@
 
 BOX_DEV = 64
 SWEEPS = 4
+SENT = 6
 NT = (((1,), (1,)), ((), ()))
 F32 = jnp.float32
 BF16 = jnp.bfloat16
@@ -36,7 +37,7 @@
     return lax.dot_general(a, b, NT, preferred_element_type=F32)
 
 
-def pack_kernel(size_z, step, sens, weight, device, cell, owner, slot, out, tri, seen):
+def pack_kernel(step, sens, weight, device, cell, owner, slot, out, tri, seen):
     targets, fields, capacity = out.shape
     rows = sens.shape[1]
     out[...] = jnp.zeros_like(out)
@@ -54,15 +55,13 @@
         rank = jnp.sum(jnp.where(chosen, before, 0.0), axis=0, keepdims=True).astype(jnp.int32)
         seen[...] = seen[...] + jnp.sum(jnp.where(chosen, 1.0, 0.0), axis=1, keepdims=True)
         place = one_hot(matches(capacity, rank))
-        cells = cell[:, span]
         payload = jnp.concatenate(
             [
                 sens[:, span],
+                cell[:, span].astype(F32),
                 weight[:, span],
-                (cells % size_z).astype(F32),
-                (cells // size_z).astype(F32),
-                owner[:, span].astype(F32),
-                slot[:, span].astype(F32),
+                (owner[:, span] * BOX_DEV + slot[:, span]).astype(F32),
+                jnp.zeros((fields - SENT, step), F32),
             ],
             axis=0,
         )
@@ -80,10 +79,10 @@
     lax.fori_loop(0, rows // step, block, 0)
 
 
-def pack_rows(size_z, devices, capacity, sens, weight, device, cell, owner, slot):
-    step = min(512, sens.shape[1])
+def pack_rows(devices, capacity, sens, weight, device, cell, owner, slot):
+    step = min(1024, sens.shape[1])
     return pl.pallas_call(
-        functools.partial(pack_kernel, size_z, step),
+        functools.partial(pack_kernel, step),
         out_shape=jax.ShapeDtypeStruct((devices, 8, capacity), F32),
         in_specs=[pl.BlockSpec(memory_space=pltpu.VMEM)] * 6,
         out_specs=pl.BlockSpec(memory_space=pltpu.VMEM),
@@ -93,7 +92,7 @@
 
 
 def joined(ref):
-    return jnp.concatenate([ref[i] for i in range(ref.shape[0])], axis=1)
+    return jnp.concatenate([ref[i, :SENT] for i in range(ref.shape[0])], axis=1)
 
 
 def scatter_kernel(arrived, load, total):
@@ -104,8 +103,9 @@
         total[...] = jnp.zeros_like(total)
 
     block = joined(arrived)
-    at_z = matches(size_z, block[4:5].astype(jnp.int32))
-    at_xy = one_hot(matches(size_xy, block[5:6].astype(jnp.int32)))
+    cell = block[3:4].astype(jnp.int32)
+    at_z = matches(size_z, cell % size_z)
+    at_xy = one_hot(matches(size_xy, cell // size_z))
     pairs = [two_terms(block[k : k + 1]) for k in range(parts)]
     terms = [scaled(at_z, hi) for hi, lo in pairs] + [scaled(at_z, lo) for hi, lo in pairs]
     product = dot_nt(jnp.concatenate(terms, axis=0), at_xy)
@@ -144,15 +144,17 @@
             terms[(parts + k) * size_z : (parts + k + 1) * size_z] = lo.astype(BF16)
 
     block = joined(arrived)
-    at_z = matches(size_z, block[4:5].astype(jnp.int32))
-    at_xy = one_hot(matches(size_xy, block[5:6].astype(jnp.int32)))
+    cell = block[3:4].astype(jnp.int32)
+    at_z = matches(size_z, cell % size_z)
+    at_xy = one_hot(matches(size_xy, cell // size_z))
     columns = jnp.dot(terms[...], at_xy, preferred_element_type=F32)
-    at_owner = one_hot(matches(devices, block[6:7].astype(jnp.int32)))
-    at_slot = matches(BOX_DEV, block[7:8].astype(jnp.int32))
+    box = block[5:6].astype(jnp.int32)
+    at_owner = one_hot(matches(devices, box // BOX_DEV))
+    at_slot = matches(BOX_DEV, box % BOX_DEV)
     for k in range(parts):
         column = columns[k * size_z : (k + 1) * size_z]
         column = column + columns[(parts + k) * size_z : (parts + k + 1) * size_z]
-        value = jnp.sum(jnp.where(at_z, column, 0.0), axis=0, keepdims=True) * block[3:4]
+        value = jnp.sum(jnp.where(at_z, column, 0.0), axis=0, keepdims=True) * block[4:5]
         hi, lo = two_terms(value)
         part = dot_nt(at_owner, scaled(at_slot, hi)) + dot_nt(at_owner, scaled(at_slot, lo))
         boxes[:, k * BOX_DEV : (k + 1) * BOX_DEV] += part
@@ -321,7 +323,7 @@
     )(load, stiffness, anchor, coupling)
 
 
-def exchange_kernel(send, recv, send_sem, recv_sem, own_sem):
+def exchange_kernel(live, send, recv, send_sem, recv_sem, own_sem):
     count = send.shape[0]
     width = lax.axis_size("gy")
     me = lax.axis_index("gx") * width + lax.axis_index("gy")
@@ -340,8 +342,8 @@
     def copy(step, source, landing):
         peer = (me + step) % count
         return pltpu.make_async_remote_copy(
-            src_ref=send.at[source],
-            dst_ref=recv.at[landing],
+            src_ref=send.at[source, pl.ds(0, live)],
+            dst_ref=recv.at[landing, pl.ds(0, live)],
             send_sem=send_sem.at[step],
             recv_sem=recv_sem.at[step],
             device_id=device(peer),
@@ -353,7 +355,7 @@
         return carry
 
     lax.fori_loop(1, count, start, 0)
-    own = pltpu.make_async_copy(send.at[me], recv.at[me], own_sem)
+    own = pltpu.make_async_copy(send.at[me, pl.ds(0, live)], recv.at[me, pl.ds(0, live)], own_sem)
     own.start()
 
     def finish(step, carry):
@@ -365,10 +367,10 @@
     own.wait()
 
 
-def exchange(blocks, number):
+def exchange(blocks, live, number):
     count = blocks.shape[0]
     return pl.pallas_call(
-        exchange_kernel,
+        functools.partial(exchange_kernel, live),
         out_shape=jax.ShapeDtypeStruct(blocks.shape, F32),
         in_specs=[pl.BlockSpec(memory_space=pltpu.VMEM)],
         out_specs=pl.BlockSpec(memory_space=pltpu.VMEM),
@@ -394,13 +396,13 @@
     capacity = 2 * row_count // devices
     size_x, size_y, size_z = stiffness.shape
     size_xy = size_x * size_y
-    group = max(1, min(devices, 512 // capacity))
+    assert size_xy * size_z <= 2**17 and devices * BOX_DEV <= 2**17
+    group = max(1, min(devices, 1024 // capacity))
 
     def row(values):
         return values.reshape(1, row_count)
 
     packed = pack_rows(
-        size_z,
         devices,
         capacity,
         sensitivity,
@@ -410,12 +412,12 @@
         row(box_owner),
         row(box_slot),
     )
-    arrived = exchange(packed, 1)
+    arrived = exchange(packed, SENT, 1)
     load = scatter_rows(arrived, group, size_xy, size_z)
     load = load.reshape(3, size_x, size_y, size_z)
     adjoint = solve_sweeps(load, stiffness, anchor, coupling)
     partial = gather_rows(arrived, group, adjoint.reshape(3, size_xy, size_z))
-    partial = exchange(partial.reshape(devices, 1, 3 * BOX_DEV), 2)
+    partial = exchange(partial.reshape(devices, 1, 3 * BOX_DEV), 1, 2)
     box_gradient = jnp.sum(partial, axis=(0, 1)).reshape(3, BOX_DEV)
     return (adjoint, box_gradient)
 

time: 148 us -> 136 us (0.919)
  Pallas kernels: 142 us -> 131 us
    pallas_call x3, Pallas kernels: 41.8 us -> 37.7 us  [the longest x2 26.8 us: exchange(): pl.pallas_call(functools.partial(exchange_kernel, live), out_shape=jax.Sh...]
    pallas_call x1, Pallas kernels: 42.2 us -> 38.7 us  [gather_rows(): pl.pallas_call(gather_kernel, grid=(devices // group,), out_shape=jax.Sha...]
    pallas_call x1, Pallas kernels: 35.6 us -> 32.1 us  [scatter_rows(): pl.pallas_call(scatter_kernel, grid=(devices // group,), out_shape=jax.Sh...]
where the time goes in v3:
time: 136 us
  Pallas kernels  131 us (96%)
  local copies, waits for them, and re-layouts  3.19 us (2%)
    pallas_call x1, Pallas kernels, gather_rows(): pl.pallas_call(gather_kernel, grid=(devices // group,), out_shape=jax.Sha...  38.7 us
    pallas_call x1, Pallas kernels, scatter_rows(): pl.pallas_call(scatter_kernel, grid=(devices // group,), out_shape=jax.Sh...  32.1 us
    pallas_call x2, Pallas kernels, exchange(): pl.pallas_call(functools.partial(exchange_kernel, live), out_shape=jax.Sh...  26.8 us
    pallas_call x1, Pallas kernels, solve_sweeps(): pl.pallas_call(sweep_kernel, out_shape=jax.ShapeDtypeStruct(load.shape, F...  22.3 us
    pallas_call x1, Pallas kernels, pack_rows(): pl.pallas_call(functools.partial(pack_kernel, step), out_shape=jax.ShapeD...  10.9 us

profile of v3, /device:TPU:0, one launch (start us, length us, event | category | flops | bytes accessed | tf_op | source)
XLA Modules:
  0.0 135.5 jit_solution(13006453911097069828)
XLA Ops:
  0.6 10.9 %pack_rows.1.send = f32[32,8,512]{2,1,0:T(8,128)} custom-call(f32[3,8192]{1,0:T(4,128)} %sens.1, f32[1,8192]{1,0:T(1,128)} %bitcast.9, s32[1,8192]{1,0:T(1,128)} %bitcast.10, s32[1,8192]{1,0:T(1,128)} %bitcast.11, s32[1,8192]{1,0:T(1,128)} %bitcast.12, s32[1,8192]{1,0:T(1,128)} %bitcast.13), custom_call_target="tpu_custom_call" | custom-call | tf_op jit(solution)/shard_map/pack_rows/pallas_call | solution.py:84
  11.5 16.3 %exchange_1.1.arrived = f32[32,8,512]{2,1,0:T(8,128)} custom-call(f32[32,8,512]{2,1,0:T(8,128)} %pack_rows.1.send), custom_call_target="tpu_custom_call" | custom-call | tf_op jit(solution)/shard_map/exchange_1/pallas_call | solution.py:372
  27.8 32.1 %scatter_rows.1 = f32[3,512,256]{2,1,0:T(8,128)} custom-call(f32[32,8,512]{2,1,0:T(8,128)} %exchange_1.1.arrived), custom_call_target="tpu_custom_call" | custom-call | tf_op jit(solution)/shard_map/scatter_rows/pallas_call | solution.py:123
  59.9 22.3 %sweeps.1 = f32[3,16,32,256]{3,2,1,0:T(8,128)} custom-call(f32[3,16,32,256]{3,2,1,0:T(8,128)} %bitcast.8, f32[16,32,256]{2,1,0:T(8,128)} %stiff.1, f32[3,16,32,256]{3,2,1,0:T(8,128)} %anchor.1, f32[9,16,32,256]{3,2,1,0:T(8,128)} %coupling.1), custom_call_target="tpu_custom_call" | custom-call | tf_op jit(solution)/shard_map/sweeps/pallas_call | solution.py:308
  82.2 0.0 copy-start
  82.3 38.7 %gather_rows.1 = f32[32,192]{1,0:T(8,128)} custom-call(f32[32,8,512]{2,1,0:T(8,128)} %exchange_1.1.arrived, f32[3,512,256]{2,1,0:T(8,128)} %bitcast.7), custom_call_target="tpu_custom_call" | custom-call | tf_op jit(solution)/shard_map/gather_rows/pallas_call | solution.py:166
  121.0 1.4 %reshape.38.send = f32[32,1,192]{2,1,0:T(1,128)} reshape(f32[32,192]{1,0:T(8,128)} %gather_rows.1) | data formatting | bytes 49152 | tf_op jit(solution)/shard_map/reshape | solution.py:420
  122.4 10.5 %exchange_2.1 = f32[32,1,192]{2,1,0:T(1,128)} custom-call(f32[32,1,192]{2,1,0:T(1,128)} %reshape.38.send), custom_call_target="tpu_custom_call" | custom-call | tf_op jit(solution)/shard_map/exchange_2/pallas_call | solution.py:372
  132.9 0.8 reduce_sum.9
  133.7 0.7 reshape.39
  134.4 0.0 copy-done
  134.4 1.1 copy.12
Async XLA Ops:
  82.2 52.1 %copy-start = (f32[3,16,32,256]{3,2,1,0:T(8,128)S(1)}, f32[3,16,32,256]{3,2,1,0:T(8,128)}, u32[]{:S(2)}) copy-start(f32[3,16,32,256]{3,2,1,0:T(8,128)} %sweeps.1) | copy-start | bytes 4718596

commit v4 on v3

--- a/solution.py
+++ b/solution.py
@@ -80,7 +80,7 @@
 
 
 def pack_rows(devices, capacity, sens, weight, device, cell, owner, slot):
-    step = min(1024, sens.shape[1])
+    step = min(2048, sens.shape[1])
     return pl.pallas_call(
         functools.partial(pack_kernel, step),
         out_shape=jax.ShapeDtypeStruct((devices, 8, capacity), F32),
@@ -397,7 +397,7 @@
     size_x, size_y, size_z = stiffness.shape
     size_xy = size_x * size_y
     assert size_xy * size_z <= 2**17 and devices * BOX_DEV <= 2**17
-    group = max(1, min(devices, 1024 // capacity))
+    group = max(1, min(devices, 2048 // capacity))
 
     def row(values):
         return values.reshape(1, row_count)

time: 136 us -> 134 us (0.985)
  Pallas kernels: 131 us -> 129 us
    pallas_call x1, Pallas kernels: 10.9 us -> 13.3 us  [pack_rows(): pl.pallas_call(functools.partial(pack_kernel, step), out_shape=jax.ShapeD...]
    pallas_call x1, Pallas kernels: 38.7 us -> 36.3 us  [gather_rows(): pl.pallas_call(gather_kernel, grid=(devices // group,), out_shape=jax.Sha...]
    pallas_call x1, Pallas kernels: 32.1 us -> 30.3 us  [scatter_rows(): pl.pallas_call(scatter_kernel, grid=(devices // group,), out_shape=jax.Sh...]
where the time goes in v4:
time: 134 us
  Pallas kernels  129 us (96%)
  local copies, waits for them, and re-layouts  3.19 us (2%)
    pallas_call x1, Pallas kernels, gather_rows(): pl.pallas_call(gather_kernel, grid=(devices // group,), out_shape=jax.Sha...  36.3 us
    pallas_call x1, Pallas kernels, scatter_rows(): pl.pallas_call(scatter_kernel, grid=(devices // group,), out_shape=jax.Sh...  30.3 us
    pallas_call x2, Pallas kernels, exchange(): pl.pallas_call(functools.partial(exchange_kernel, live), out_shape=jax.Sh...  26.8 us
    pallas_call x1, Pallas kernels, solve_sweeps(): pl.pallas_call(sweep_kernel, out_shape=jax.ShapeDtypeStruct(load.shape, F...  22.3 us
    pallas_call x1, Pallas kernels, pack_rows(): pl.pallas_call(functools.partial(pack_kernel, step), out_shape=jax.ShapeD...  13.3 us

profile of v4, /device:TPU:0, one launch (start us, length us, event | category | flops | bytes accessed | tf_op | source)
XLA Modules:
  0.0 133.8 jit_solution(15552015866364923186)
XLA Ops:
  0.6 13.3 %pack_rows.1.send = f32[32,8,512]{2,1,0:T(8,128)} custom-call(f32[3,8192]{1,0:T(4,128)} %sens.1, f32[1,8192]{1,0:T(1,128)} %bitcast.9, s32[1,8192]{1,0:T(1,128)} %bitcast.10, s32[1,8192]{1,0:T(1,128)} %bitcast.11, s32[1,8192]{1,0:T(1,128)} %bitcast.12, s32[1,8192]{1,0:T(1,128)} %bitcast.13), custom_call_target="tpu_custom_call" | custom-call | tf_op jit(solution)/shard_map/pack_rows/pallas_call | solution.py:84
  14.0 16.3 %exchange_1.1.arrived = f32[32,8,512]{2,1,0:T(8,128)} custom-call(f32[32,8,512]{2,1,0:T(8,128)} %pack_rows.1.send), custom_call_target="tpu_custom_call" | custom-call | tf_op jit(solution)/shard_map/exchange_1/pallas_call | solution.py:372
  30.2 30.3 %scatter_rows.1 = f32[3,512,256]{2,1,0:T(8,128)} custom-call(f32[32,8,512]{2,1,0:T(8,128)} %exchange_1.1.arrived), custom_call_target="tpu_custom_call" | custom-call | tf_op jit(solution)/shard_map/scatter_rows/pallas_call | solution.py:123
  60.5 22.3 %sweeps.1 = f32[3,16,32,256]{3,2,1,0:T(8,128)} custom-call(f32[3,16,32,256]{3,2,1,0:T(8,128)} %bitcast.8, f32[16,32,256]{2,1,0:T(8,128)} %stiff.1, f32[3,16,32,256]{3,2,1,0:T(8,128)} %anchor.1, f32[9,16,32,256]{3,2,1,0:T(8,128)} %coupling.1), custom_call_target="tpu_custom_call" | custom-call | tf_op jit(solution)/shard_map/sweeps/pallas_call | solution.py:308
  82.9 0.0 copy-start
  82.9 36.3 %gather_rows.1 = f32[32,192]{1,0:T(8,128)} custom-call(f32[32,8,512]{2,1,0:T(8,128)} %exchange_1.1.arrived, f32[3,512,256]{2,1,0:T(8,128)} %bitcast.7), custom_call_target="tpu_custom_call" | custom-call | tf_op jit(solution)/shard_map/gather_rows/pallas_call | solution.py:166
  119.2 1.4 %reshape.38.send = f32[32,1,192]{2,1,0:T(1,128)} reshape(f32[32,192]{1,0:T(8,128)} %gather_rows.1) | data formatting | bytes 49152 | tf_op jit(solution)/shard_map/reshape | solution.py:420
  120.6 10.5 %exchange_2.1 = f32[32,1,192]{2,1,0:T(1,128)} custom-call(f32[32,1,192]{2,1,0:T(1,128)} %reshape.38.send), custom_call_target="tpu_custom_call" | custom-call | tf_op jit(solution)/shard_map/exchange_2/pallas_call | solution.py:372
  131.2 0.8 reduce_sum.9
  132.0 0.7 reshape.39
  132.6 0.0 copy-done
  132.6 1.1 copy.12
Async XLA Ops:
  82.9 49.8 %copy-start = (f32[3,16,32,256]{3,2,1,0:T(8,128)S(1)}, f32[3,16,32,256]{3,2,1,0:T(8,128)}, u32[]{:S(2)}) copy-start(f32[3,16,32,256]{3,2,1,0:T(8,128)} %sweeps.1) | copy-start | bytes 4718596
